TPU v7x, 32 devices: a whole 2x2x4 slice. The times are simulated.
32 devices in a mesh: wide: 16 (over z, x, core), narrow: 2 (over y).
Axes of the slice: x: 2, y: 2, z: 4, core: 2. Of those that a mesh axis runs over, the one named last changes fastest.
Arguments:
- layer_in: bfloat16 [128, 256, 768], P(('wide', 'narrow')), may hold values from -6 to 6
- segment_ids: int32 [128, 256], P(('wide', 'narrow')), may hold values from 0 to 31, as said below
- live_mask: int32 [128, 256], P(('wide', 'narrow')), may hold values from 0 to 1, as said below
- expert_ids: int32 [128], P(('wide', 'narrow')), may hold values from 1 to 2
- cotangent: bfloat16 [128, 256, 768], P(('wide', 'narrow')), may hold values from -6 to 6
- norm1_gain: float32 [768], replicated, may hold values from 0.1 to 1.9
- norm1_bias: float32 [768], replicated, may hold values from -3 to 3
- q_weight: bfloat16 [768, 768], P('wide'), may hold values from -0.21875 to 0.21875
- q_bias: float32 [768], replicated, may hold values from -3 to 3
- k_weight: bfloat16 [768, 768], P('wide'), may hold values from -0.21875 to 0.21875
- v_weight: bfloat16 [768, 768], P('wide'), may hold values from -0.21875 to 0.21875
- v_bias: float32 [768], replicated, may hold values from -3 to 3
- o_weight: bfloat16 [768, 768], P('wide'), may hold values from -0.875 to 0.875
- o_bias: float32 [768], replicated, may hold values from -3 to 3
- norm2_gain: float32 [768], replicated, may hold values from 0.1 to 1.9
- norm2_bias: float32 [768], replicated, may hold values from -3 to 3
- in_weight: bfloat16 [768, 3072], P('wide'), may hold values from -0.21875 to 0.21875
- in_bias: float32 [3072], replicated, may hold values from -3 to 3
- out_weight: bfloat16 [3072, 768], P('wide'), may hold values from -0.109375 to 0.109375
- out_bias: float32 [768], replicated, may hold values from -3 to 3
Outputs:
- layer_out: bfloat16 [128, 256, 768], P(('wide', 'narrow'))
- input_grad: bfloat16 [128, 256, 768], P(('wide', 'narrow'))
- counts: int32 [3], replicated
- norm1_gain_grad: float32 [768], replicated
- norm1_bias_grad: float32 [768], replicated
- q_weight_grad: float32 [768, 768], P('wide')
- q_bias_grad: float32 [768], replicated
- k_weight_grad: float32 [768, 768], P('wide')
- v_weight_grad: float32 [768, 768], P('wide')
- v_bias_grad: float32 [768], replicated
- o_weight_grad: float32 [768, 768], P('wide')
- o_bias_grad: float32 [768], replicated
- norm2_gain_grad: float32 [768], replicated
- norm2_bias_grad: float32 [768], replicated
- in_weight_grad: float32 [768, 3072], P('wide')
- in_bias_grad: float32 [3072], replicated
- out_weight_grad: float32 [3072, 768], P('wide')
- out_bias_grad: float32 [768], replicated
Inputs may be any that keep to these rules, and one draw needn't show every extreme that they name: `segment_ids`: in each row the captions, 8 to 40 tokens each, lie in order and are numbered from 0; after the last caption the padding slots carry the next number. `live_mask`: the live slots of a row are a prefix of it, at least 8 of them. `expert_ids`: no row names the vision expert.
All inputs are finite; a program needn't handle non-finite values.
Results may differ from a plain program's by a relative error of at most 0.018.
Values may be sent and summed in bfloat16 or wider, within the bound.
A program may use at most 192 MiB of HBM per device.

v0:
```python
import math
import jax
import jax.numpy as jnp
from jax import lax
from jax.sharding import PartitionSpec as P

HEADS = 12
EPSILON = 1e-06
MASKED = -1e30


def norm_rows(values, gain_vec, bias_vec):
    row_mean = jnp.mean(values, axis=-1, keepdims=True)
    centred = values - row_mean
    variance = jnp.mean(centred * centred, axis=-1, keepdims=True)
    return centred * lax.rsqrt(variance + EPSILON) * gain_vec + bias_vec


def gelu_exact(values):
    return jax.nn.gelu(values, approximate=False)


def plain_product(left, right):
    return jnp.dot(left, right, preferred_element_type=jnp.float32)


def product_left_t(left, right):
    return lax.dot_general(
        left, right, (((0,), (0,)), ((), ())), preferred_element_type=jnp.float32
    )


def product_right_t(left, right):
    return lax.dot_general(
        left, right, (((1,), (1,)), ((), ())), preferred_element_type=jnp.float32
    )


def allowed_pairs(seg_rows, live_rows):
    slot_total = seg_rows.shape[-1]
    row_pos = lax.broadcasted_iota(jnp.int32, (slot_total, slot_total), 0)
    col_pos = lax.broadcasted_iota(jnp.int32, (slot_total, slot_total), 1)
    same_seg = seg_rows[:, :, None] == seg_rows[:, None, :]
    return (same_seg & ((live_rows[:, None, :] > 0) | (row_pos == col_pos)[None]))[:, None]


def masked_scores(query_heads, key_heads, seg_rows, live_rows):
    raw_scores = (
        jnp.einsum("gqhe,gkhe->ghqk", query_heads, key_heads, preferred_element_type=jnp.float32)
        * 0.125
    )
    return jnp.where(allowed_pairs(seg_rows, live_rows), raw_scores, MASKED)


def attend_block(pieces):
    query_heads, key_heads, value_heads, seg_rows, live_rows = pieces
    scores = masked_scores(query_heads, key_heads, seg_rows, live_rows)
    row_top = jnp.max(scores, axis=-1, keepdims=True)
    exp_terms = jnp.exp(scores - row_top)
    row_total = jnp.sum(exp_terms, axis=-1, keepdims=True)
    attn_probs = (exp_terms / row_total).astype(jnp.bfloat16)
    mixed_heads = jnp.einsum(
        "ghqk,gkhe->gqhe", attn_probs, value_heads, preferred_element_type=jnp.float32
    )
    return (mixed_heads.astype(jnp.bfloat16), row_top + jnp.log(row_total))


def attend_back(pieces):
    query_heads, key_heads, value_heads, seg_rows, live_rows, log_total, grad_mixed = pieces
    scores = masked_scores(query_heads, key_heads, seg_rows, live_rows)
    attn_probs = jnp.exp(scores - log_total)
    grad_probs = jnp.einsum(
        "gqhe,gkhe->ghqk", grad_mixed, value_heads, preferred_element_type=jnp.float32
    )
    inner_sum = jnp.sum(grad_probs * attn_probs, axis=-1, keepdims=True)
    grad_scores = (attn_probs * (grad_probs - inner_sum)).astype(jnp.bfloat16)
    grad_query = (
        jnp.einsum("ghqk,gkhe->gqhe", grad_scores, key_heads, preferred_element_type=jnp.float32)
        * 0.125
    ).astype(jnp.bfloat16)
    grad_keys = (
        jnp.einsum("ghqk,gqhe->gkhe", grad_scores, query_heads, preferred_element_type=jnp.float32)
        * 0.125
    ).astype(jnp.bfloat16)
    grad_values = jnp.einsum(
        "ghqk,gqhe->gkhe",
        attn_probs.astype(jnp.bfloat16),
        grad_mixed,
        preferred_element_type=jnp.float32,
    ).astype(jnp.bfloat16)
    return (grad_query, grad_keys, grad_values)


def body(
    layer_in,
    segment_ids,
    live_mask,
    expert_ids,
    cotangent,
    norm1_gain,
    norm1_bias,
    q_weight,
    q_bias,
    k_weight,
    v_weight,
    v_bias,
    o_weight,
    o_bias,
    norm2_gain,
    norm2_bias,
    in_weight,
    in_bias,
    out_weight,
    out_bias,
):
    row_local, slot_total, width_all = layer_in.shape
    head_dim = width_all // HEADS
    group_rows = math.gcd(row_local, max(1, 512 // slot_total))
    block_total = row_local // group_rows
    token_total = row_local * slot_total
    live_tokens = jnp.sum(live_mask, axis=1)
    local_counts = jnp.stack(
        [jnp.sum(jnp.where(expert_ids == expert, live_tokens, 0)) for expert in range(3)]
    )
    counts = lax.psum(local_counts, ("wide", "narrow"))
    count_float = counts.astype(jnp.float32)
    own_count = jnp.where(expert_ids == 1, count_float[1], count_float[2])
    row_scale = (count_float[1] + count_float[2]) / (2.0 * own_count)

    def heads_blocks(values):
        return values.reshape(block_total, group_rows, slot_total, HEADS, head_dim)

    seg_blocks = segment_ids.reshape(block_total, group_rows, slot_total)
    live_blocks = live_mask.reshape(block_total, group_rows, slot_total)
    x_rows = layer_in.astype(jnp.float32).reshape(token_total, width_all)
    normed_one = norm_rows(x_rows, norm1_gain, norm1_bias).astype(jnp.bfloat16)
    full_q, full_k, full_v, full_o = (
        lax.all_gather(q_weight, "wide", axis=0, tiled=True),
        lax.all_gather(k_weight, "wide", axis=0, tiled=True),
        lax.all_gather(v_weight, "wide", axis=0, tiled=True),
        lax.all_gather(o_weight, "wide", axis=0, tiled=True),
    )
    query_act = (plain_product(normed_one, full_q) + q_bias).astype(jnp.bfloat16)
    key_act = plain_product(normed_one, full_k).astype(jnp.bfloat16)
    value_act = (plain_product(normed_one, full_v) + v_bias).astype(jnp.bfloat16)
    mixed_blocks, log_total = lax.map(
        attend_block,
        (
            heads_blocks(query_act),
            heads_blocks(key_act),
            heads_blocks(value_act),
            seg_blocks,
            live_blocks,
        ),
    )
    mixed_act = mixed_blocks.reshape(token_total, width_all)
    residual = x_rows + plain_product(mixed_act, full_o) + o_bias
    normed_two = norm_rows(residual, norm2_gain, norm2_bias).astype(jnp.bfloat16)
    full_in, full_out = (
        lax.all_gather(in_weight, "wide", axis=0, tiled=True),
        lax.all_gather(out_weight, "wide", axis=0, tiled=True),
    )
    pre_act = plain_product(normed_two, full_in) + in_bias
    hidden = gelu_exact(pre_act).astype(jnp.bfloat16)
    result = residual + plain_product(hidden, full_out) + out_bias
    layer_out = result.astype(jnp.bfloat16).reshape(row_local, slot_total, width_all)
    token_scale = (live_mask.astype(jnp.float32) * row_scale[:, None]).reshape(token_total, 1)
    grad_y = cotangent.astype(jnp.float32).reshape(token_total, width_all) * token_scale
    grad_branch = grad_y.astype(jnp.bfloat16)
    back_in, back_out = (
        lax.all_gather(in_weight, "wide", axis=0, tiled=True),
        lax.all_gather(out_weight, "wide", axis=0, tiled=True),
    )
    grad_hidden = product_right_t(grad_branch, back_out)
    gelu_pull = jax.vjp(gelu_exact, pre_act)[1]
    grad_pre = gelu_pull(grad_hidden)[0].astype(jnp.bfloat16)
    out_weight_grad = product_left_t(hidden, grad_branch)
    out_bias_grad = jnp.sum(grad_branch.astype(jnp.float32), axis=0)
    in_weight_grad = product_left_t(normed_two, grad_pre)
    in_bias_grad = jnp.sum(grad_pre.astype(jnp.float32), axis=0)
    grad_normed_two = product_right_t(grad_pre, back_in)
    norm_two_pull = jax.vjp(norm_rows, residual, norm2_gain, norm2_bias)[1]
    grad_resid_norm, norm2_gain_grad, norm2_bias_grad = norm_two_pull(grad_normed_two)
    grad_resid = grad_y + grad_resid_norm
    grad_attn = grad_resid.astype(jnp.bfloat16)
    back_q, back_k, back_v, back_o = (
        lax.all_gather(q_weight, "wide", axis=0, tiled=True),
        lax.all_gather(k_weight, "wide", axis=0, tiled=True),
        lax.all_gather(v_weight, "wide", axis=0, tiled=True),
        lax.all_gather(o_weight, "wide", axis=0, tiled=True),
    )
    o_weight_grad = product_left_t(mixed_act, grad_attn)
    o_bias_grad = jnp.sum(grad_attn.astype(jnp.float32), axis=0)
    grad_mixed = product_right_t(grad_attn, back_o).astype(jnp.bfloat16)
    grad_query, grad_keys, grad_values = lax.map(
        attend_back,
        (
            heads_blocks(query_act),
            heads_blocks(key_act),
            heads_blocks(value_act),
            seg_blocks,
            live_blocks,
            log_total,
            heads_blocks(grad_mixed),
        ),
    )
    grad_query = grad_query.reshape(token_total, width_all)
    grad_keys = grad_keys.reshape(token_total, width_all)
    grad_values = grad_values.reshape(token_total, width_all)
    q_weight_grad = product_left_t(normed_one, grad_query)
    q_bias_grad = jnp.sum(grad_query.astype(jnp.float32), axis=0)
    k_weight_grad = product_left_t(normed_one, grad_keys)
    v_weight_grad = product_left_t(normed_one, grad_values)
    v_bias_grad = jnp.sum(grad_values.astype(jnp.float32), axis=0)
    grad_normed_one = (
        product_right_t(grad_query, back_q)
        + product_right_t(grad_keys, back_k)
        + product_right_t(grad_values, back_v)
    )
    norm_one_pull = jax.vjp(norm_rows, x_rows, norm1_gain, norm1_bias)[1]
    grad_x_norm, norm1_gain_grad, norm1_bias_grad = norm_one_pull(grad_normed_one)
    input_grad = (
        (grad_resid + grad_x_norm).astype(jnp.bfloat16).reshape(row_local, slot_total, width_all)
    )
    summed_vectors = lax.psum(
        (
            norm1_gain_grad,
            norm1_bias_grad,
            q_bias_grad,
            v_bias_grad,
            o_bias_grad,
            norm2_gain_grad,
            norm2_bias_grad,
            in_bias_grad,
            out_bias_grad,
        ),
        ("wide", "narrow"),
    )
    row_pieces = (
        lax.psum_scatter(
            q_weight_grad.astype(jnp.bfloat16), "wide", scatter_dimension=0, tiled=True
        ).astype(jnp.float32),
        lax.psum_scatter(
            k_weight_grad.astype(jnp.bfloat16), "wide", scatter_dimension=0, tiled=True
        ).astype(jnp.float32),
        lax.psum_scatter(
            v_weight_grad.astype(jnp.bfloat16), "wide", scatter_dimension=0, tiled=True
        ).astype(jnp.float32),
        lax.psum_scatter(
            o_weight_grad.astype(jnp.bfloat16), "wide", scatter_dimension=0, tiled=True
        ).astype(jnp.float32),
        lax.psum_scatter(
            in_weight_grad.astype(jnp.bfloat16), "wide", scatter_dimension=0, tiled=True
        ).astype(jnp.float32),
        lax.psum_scatter(
            out_weight_grad.astype(jnp.bfloat16), "wide", scatter_dimension=0, tiled=True
        ).astype(jnp.float32),
    )
    row_pieces = (
        lax.psum(row_pieces[0].astype(jnp.bfloat16), "narrow").astype(jnp.float32),
        lax.psum(row_pieces[1].astype(jnp.bfloat16), "narrow").astype(jnp.float32),
        lax.psum(row_pieces[2].astype(jnp.bfloat16), "narrow").astype(jnp.float32),
        lax.psum(row_pieces[3].astype(jnp.bfloat16), "narrow").astype(jnp.float32),
        lax.psum(row_pieces[4].astype(jnp.bfloat16), "narrow").astype(jnp.float32),
        lax.psum(row_pieces[5].astype(jnp.bfloat16), "narrow").astype(jnp.float32),
    )
    return (
        layer_out,
        input_grad,
        counts,
        summed_vectors[0],
        summed_vectors[1],
        row_pieces[0],
        summed_vectors[2],
        row_pieces[1],
        row_pieces[2],
        summed_vectors[3],
        row_pieces[3],
        summed_vectors[4],
        summed_vectors[5],
        summed_vectors[6],
        row_pieces[4],
        summed_vectors[7],
        row_pieces[5],
        summed_vectors[8],
    )


def solution(mesh):
    placed = (
        P(("wide", "narrow"), None, None),
        P(("wide", "narrow"), None),
        P(("wide", "narrow"), None),
        P(("wide", "narrow")),
        P(("wide", "narrow"), None, None),
        P(),
        P(),
        P("wide", None),
        P(),
        P("wide", None),
        P("wide", None),
        P(),
        P("wide", None),
        P(),
        P(),
        P(),
        P("wide", None),
        P(),
        P("wide", None),
        P(),
    )
    return jax.shard_map(
        body,
        mesh=mesh,
        in_specs=placed,
        out_specs=(
            P(("wide", "narrow"), None, None),
            P(("wide", "narrow"), None, None),
            P(),
            P(),
            P(),
            P("wide", None),
            P(),
            P("wide", None),
            P("wide", None),
            P(),
            P("wide", None),
            P(),
            P(),
            P(),
            P("wide", None),
            P(),
            P("wide", None),
            P(),
        ),
        check_vma=False,
    )
```

profile of v0, /device:TPU:0, one launch (start us, length us, event | category | flops | bytes accessed | tf_op | source)
XLA Modules:
  0.0 776.0 jit_solution(13493928599702478998)
XLA Ops:
  18.4 42.4 %psum.112 = s32[3]{0:T(128)S(1)} all-reduce(s32[3]{0:T(128)S(1)} %pad_add_fusion), channel_id=1, replica_groups=mesh['wide'=16,'narrow'=2] {'wide','narrow'}, use_global_device_ids=true, to_apply=%region_12.13 | all-reduce | flops 3 | bytes 24 | tf_op jit(solution)/shard_map/psum | solution.py:125
  76.4 14.6 %all-gather.9.cloned.1.call-done = bf16[768,768]{1,0:T(8,128)(2,1)} async-done(((bf16[48,768]{1,0:T(8,128)(2,1)}), bf16[768,768]{1,0:T(8,128)(2,1)}) %all-gather.9.cloned.1.call-update) | async-done | bytes 1179664 | tf_op jit(solution)/shard_map/all_gather | solution.py:138
  98.5 32.1 %all-gather.11.cloned.1.call-done = bf16[768,768]{1,0:T(8,128)(2,1)} async-done(((bf16[48,768]{1,0:T(8,128)(2,1)}), bf16[768,768]{1,0:T(8,128)(2,1)}) %all-gather.11.cloned.1.call-update) | async-done | bytes 1179664 | tf_op jit(solution)/shard_map/all_gather | solution.py:139
  130.6 4.3 convolution_convert_fusion.3
  146.4 16.6 %while.26 = (s32[]{:T(128)}, bf16[2,2,256,12,64]{2,1,0,4,3:T(2,128)(2,1)}, f32[2,2,12,256,1]{3,2,1,4,0:T(8,128)}, bf16[2,2,256,12,64]{2,4,3,1,0:T(8,128)(2,1)}, ...) while((s32[]{:T(128)}, ...), condition=%wide.region_5.6_spmd, body=%wide.region_2.5_spmd.sunk | while | flops 422373888 | bytes 30772356 | solution.py:146
  176.2 48.2 %all-gather.15.cloned.1.call-done = bf16[768,3072]{1,0:T(8,128)(2,1)} async-done(((bf16[48,3072]{1,0:T(8,128)(2,1)}), bf16[768,3072]{1,0:T(8,128)(2,1)}) %all-gather.15.cloned.1.call-update) | async-done | bytes 4718608 | tf_op jit(solution)/shard_map/all_gather | solution.py:160
  224.4 38.2 %multiply_convert_fusion.3 = (bf16[1024,3072]{1,0:T(8,128)(2,1)}, f32[1024,3072]{1,0:T(8,128)}, f32[1024,3072]{1,0:T(8,128)}) fusion(f32[3072]{0:T(1024)S(1)} %copy-done.55, bf16[768,3072]{1,0:T(8,128)(2,1)} %all-gather.15.cloned.1.call-done, f32[1024,768]{1,0:T(8,128)} %copy-done.12, f32[768]{0:T(1024)S(1)} %copy-done.59, f32[768]{0:T(1024)S(1)} %copy-done.48, ...), kind=kOutput, calls=%fused_computation.74 | convolution fusion | flops 5043388416 | bytes 39348224 | tf_op jit(solution)/shard_map/dot_general | solution.py:24
  262.6 15.8 %all-gather.17.cloned.1.call-done = bf16[3072,768]{1,0:T(8,128)(2,1)} async-done(((bf16[192,768]{1,0:T(8,128)(2,1)}), bf16[3072,768]{1,0:T(8,128)(2,1)}) %all-gather.17.cloned.1.call-update) | async-done | bytes 4718608 | tf_op jit(solution)/shard_map/all_gather | solution.py:161
  278.4 19.0 %convert_reduce_fusion = (f32[3072]{0:T(1024)}, bf16[1024,3072]{1,0:T(8,128)(2,1)}) fusion(f32[1024,3072]{1,0:T(8,128)} %get-tuple-element.231, bf16[1024,768]{1,0:T(8,128)(2,1)} %fusion.76, bf16[3072,768]{1,0:T(8,128)(2,1)} %all-gather.17.cloned.1.call-done, f32[1024,3072]{1,0:T(8,128)} %get-tuple-element.244, f32[3072]{0:T(1024)S(1)} %copy-done.55), kind=kOutput, calls=%fused_computation.72 | convolution fusion | flops 4885312512 | bytes 37773312 | tf_op jit(solution)/shard_map/dot_general | solution.py:34
  297.4 10.2 %multiply_reduce_fusion.1 = (f32[768]{0:T(1024)}, f32[1024]{0:T(1024)S(1)}, f32[768]{0:T(1024)}, f32[1024,768]{1,0:T(8,128)S(1)}) fusion(f32[1024,768]{1,0:T(8,128)S(1)} %copy-done.13, f32[1024]{0:T(1024)S(1)} %fusion.78, f32[1024]{0:T(1024)S(1)} %broadcast_multiply_fusion, f32[768]{0:T(1024)S(1)} %copy-done.48, ...), kind=kOutput, calls=%fused_computation.115 | convolution fusion | flops 4838126592 | bytes 17323008 | tf_op jit(solution)/shard_map/dot_general | solution.py:34
  327.7 30.1 %while.27 = (s32[]{:T(128)}, bf16[2,2,256,12,64]{2,4,3,1,0:T(8,128)(2,1)}, bf16[2,2,256,12,64]{2,1,0,4,3:T(2,128)(2,1)}, bf16[2,2,256,12,64]{2,4,3,1,0:T(8,128)(...) while((s32[]{:T(128)}, ...), condition=%wide.region_17.18_spmd, body=%wide.region_15.17_spmd.sunk | while | flops 1032645120 | bytes 109375376 | solution.py:195
  362.2 4.4 convolution_convert_fusion.5
  370.7 4.6 convolution_convert_fusion.7
  377.7 4.5 convolution_convert_fusion.6
  382.3 10.0 %convolution_convert_fusion.1 = bf16[768,3072]{1,0:T(8,128)(2,1)} fusion(bf16[1024,3072]{1,0:T(8,128)(2,1)} %get-tuple-element.248, f32[1024,768]{1,0:T(8,128)S(1)} %copy-done.14, f32[768]{0:T(1024)S(1)} %copy-done.60, f32[768]{0:T(1024)S(1)} %copy-done.48, f32[1024]{0:T(1024)S(1)} %fusion.78, f32[1024]{0:T(1024)S(1)} %broadcast_multiply_fusion), kind=kOutput, calls=%fused_computation.89 | convolution fusion | flops 4838129664 | bytes 14170112 | tf_op jit(solution)/shard_map/dot_general | solution.py:28
  393.7 9.9 %convolution_convert_fusion = bf16[3072,768]{1,0:T(8,128)(2,1)} fusion(bf16[1024,3072]{1,0:T(8,128)(2,1)} %get-tuple-element.230, bf16[1024,768]{1,0:T(8,128)(2,1)S(1)} %copy-done.24), kind=kOutput, calls=%fused_computation.88 | convolution fusion | flops 4834197504 | bytes 12582912 | tf_op jit(solution)/shard_map/dot_general | solution.py:28
  417.6 6.1 add_convert_fusion.2
  423.8 8.8 %reduce-scatter.11.cloned.1.call-done = bf16[48,768]{1,0:T(8,128)(2,1)} async-done(((bf16[768,768]{1,0:T(8,128)(2,1)}), bf16[48,768]{1,0:T(8,128)(2,1)}) %reduce-scatter.11.cloned.1.call-update) | async-done | bytes 73744 | tf_op jit(solution)/shard_map/reduce_scatter | solution.py:246
  432.5 60.8 %reduce-scatter.7.cloned.1.call-done = bf16[48,768]{1,0:T(8,128)(2,1)} async-done(((bf16[768,768]{1,0:T(8,128)(2,1)}), bf16[48,768]{1,0:T(8,128)(2,1)}) %reduce-scatter.7.cloned.1.call-update) | async-done | bytes 73744 | tf_op jit(solution)/shard_map/reduce_scatter | solution.py:240
  493.3 60.5 %reduce-scatter.9.cloned.1.call-done = bf16[48,768]{1,0:T(8,128)(2,1)} async-done(((bf16[768,768]{1,0:T(8,128)(2,1)}), bf16[48,768]{1,0:T(8,128)(2,1)}) %reduce-scatter.9.cloned.1.call-update) | async-done | bytes 73744 | tf_op jit(solution)/shard_map/reduce_scatter | solution.py:243
  553.8 78.6 %reduce-scatter.15.cloned.1.call-done = bf16[48,3072]{1,0:T(8,128)(2,1)} async-done(((bf16[768,3072]{1,0:T(8,128)(2,1)}), bf16[48,3072]{1,0:T(8,128)(2,1)}) %reduce-scatter.15.cloned.1.call-update) | async-done | bytes 294928 | tf_op jit(solution)/shard_map/reduce_scatter | solution.py:252
  632.3 78.9 %reduce-scatter.17.cloned.1.call-done = bf16[192,768]{1,0:T(8,128)(2,1)} async-done(((bf16[3072,768]{1,0:T(8,128)(2,1)}), bf16[192,768]{1,0:T(8,128)(2,1)}) %reduce-scatter.17.cloned.1.call-update) | async-done | bytes 294928 | tf_op jit(solution)/shard_map/reduce_scatter | solution.py:255
  713.7 41.2 %all-reduce = (f32[768]{0:T(1024)}, f32[768]{0:T(1024)}, f32[768]{0:T(1024)}, f32[768]{0:T(1024)}, f32[768]{0:T(1024)}, /*index=5*/f32[768]{0:T(1024)}, f32[768]{0:T(1024)}, f32[3072]{0:T(1024)}, f32[768]{0:T(1024)}) all-reduce(f32[768]{0:T(1024)S(1)} %get-tuple-element.165, ...), channel_id=1, replica_groups=mesh['wide'=16,'narrow'=2] {'wide','narrow'}, use_global_device_ids=true, to_apply=%region_21.22 | all-reduce | flops 9216 | bytes 73728 | tf_op jit(solution)/shard_map/psum | solution.py:225
  754.9 4.5 add_convert_fusion.1
  (301 shorter events, 161.7 us)
Async XLA Ops:
  7.2 56.8 %copy-start.38 = (s32[4,256]{1,0:T(4,128)S(1)}, s32[4,256]{1,0:T(4,128)}, u32[]{:S(2)}) copy-start(s32[4,256]{1,0:T(4,128)} %param.26) | copy-start | bytes 12292
  7.2 56.9 %copy-start.32 = (f32[768]{0:T(1024)S(1)}, f32[768]{0:T(1024)}, u32[]{:S(2)}) copy-start(f32[768]{0:T(1024)} %param.29) | copy-start | bytes 9220
  7.2 56.9 %copy-start.44 = (f32[768]{0:T(1024)S(1)}, f32[768]{0:T(1024)}, u32[]{:S(2)}) copy-start(f32[768]{0:T(1024)} %param.30) | copy-start | bytes 9220
  7.3 61.0 %all-gather.7.cloned.1.call-start = ((), (), s32[]{:S(2)}) async-start(), calls=%async_computation.6 | async-start | bytes 1253376 | tf_op jit(solution)/shard_map/all_gather | solution.py:140
  8.0 83.0 %all-gather.9.cloned.1.call-start = ((), (), s32[]{:S(2)}) async-start(), calls=%async_computation.7 | async-start | bytes 1253376 | tf_op jit(solution)/shard_map/all_gather | solution.py:138
  8.7 121.9 %all-gather.11.cloned.1.call-start = ((), (), s32[]{:S(2)}) async-start(), calls=%async_computation.8 | async-start | bytes 1253376 | tf_op jit(solution)/shard_map/all_gather | solution.py:139
  9.5 160.6 %all-gather.13.cloned.1.call-start = ((), (), s32[]{:S(2)}) async-start(), calls=%async_computation.9 | async-start | bytes 1253376 | tf_op jit(solution)/shard_map/all_gather | solution.py:141
  10.1 214.4 %all-gather.15.cloned.1.call-start = ((), (), s32[]{:S(2)}) async-start(), calls=%async_computation.10 | async-start | bytes 5013504 | tf_op jit(solution)/shard_map/all_gather | solution.py:160
  10.6 267.7 %all-gather.17.cloned.1.call-start = ((), (), s32[]{:S(2)}) async-start(), calls=%async_computation.11 | async-start | bytes 5013504 | tf_op jit(solution)/shard_map/all_gather | solution.py:161
  11.2 412.6 %reduce-scatter.13.cloned.1.call-start = ((), (), s32[]{:S(2)}) async-start(), calls=%async_computation.15 | async-start | bytes 1253376 | tf_op jit(solution)/shard_map/reduce_scatter | solution.py:249
  15.7 50.9 %copy-start.36 = (f32[1024]{0:T(1024)}, f32[1024]{0:T(1024)S(1)}, u32[]{:S(2)}) copy-start(f32[1024]{0:T(1024)S(1)} %rsqrt.25) | copy-start | bytes 12292
  15.7 50.9 %copy-start.34 = (f32[1,2,4,128]{3,1,2,0:T(2,128)}, f32[1,2,4,128]{3,1,2,0:T(2,128)S(1)}, u32[]{:S(2)}) copy-start(f32[1,2,4,128]{3,1,2,0:T(2,128)S(1)} %copy.77) | copy-start | bytes 12292
  174.0 50.4 %copy-start.48 = (f32[768]{0:T(1024)S(1)}, f32[768]{0:T(1024)}, u32[]{:S(2)}) copy-start(f32[768]{0:T(1024)} %param.38) | copy-start | bytes 9220
  174.0 50.4 %copy-start.55 = (f32[3072]{0:T(1024)S(1)}, f32[3072]{0:T(1024)}, u32[]{:S(2)}) copy-start(f32[3072]{0:T(1024)} %param.41) | copy-start | bytes 36868
  174.0 50.4 %copy-start.59 = (f32[768]{0:T(1024)S(1)}, f32[768]{0:T(1024)}, u32[]{:S(2)}) copy-start(f32[768]{0:T(1024)} %param.39) | copy-start | bytes 9220
  315.0 117.6 %reduce-scatter.11.cloned.1.call-start = ((), (), s32[]{:S(2)}) async-start(), calls=%async_computation.14 | async-start | bytes 1253376 | tf_op jit(solution)/shard_map/reduce_scatter | solution.py:246
  366.7 126.7 %reduce-scatter.7.cloned.1.call-start = ((), (), s32[]{:S(2)}) async-start(), calls=%async_computation.12 | async-start | bytes 1253376 | tf_op jit(solution)/shard_map/reduce_scatter | solution.py:240
  375.3 178.5 %reduce-scatter.9.cloned.1.call-start = ((), (), s32[]{:S(2)}) async-start(), calls=%async_computation.13 | async-start | bytes 1253376 | tf_op jit(solution)/shard_map/reduce_scatter | solution.py:243
  382.2 250.1 %reduce-scatter.15.cloned.1.call-start = ((), (), s32[]{:S(2)}) async-start(), calls=%async_computation.16 | async-start | bytes 5013504 | tf_op jit(solution)/shard_map/reduce_scatter | solution.py:252
  392.3 318.9 %reduce-scatter.17.cloned.1.call-start = ((), (), s32[]{:S(2)}) async-start(), calls=%async_computation.17 | async-start | bytes 5013504 | tf_op jit(solution)/shard_map/reduce_scatter | solution.py:255
  403.7 355.7 %all-reduce.4.cloned.1.call-start = ((), (), s32[]{:S(2)}) async-start(), calls=%async_computation.18 | async-start | bytes 1769472 | tf_op jit(solution)/shard_map/psum | solution.py:260
  423.8 290.0 %copy-start.45 = (f32[3072]{0:T(1024)S(1)}, f32[3072]{0:T(1024)}, u32[]{:S(2)}) copy-start(f32[3072]{0:T(1024)} %get-tuple-element.247) | copy-start | bytes 36868
  423.8 290.0 %copy-start.50 = (f32[768]{0:T(1024)S(1)}, f32[768]{0:T(1024)}, u32[]{:S(2)}) copy-start(f32[768]{0:T(1024)} %get-tuple-element.163) | copy-start | bytes 9220
  423.8 290.0 %copy-start.51 = (f32[768]{0:T(1024)S(1)}, f32[768]{0:T(1024)}, u32[]{:S(2)}) copy-start(f32[768]{0:T(1024)} %get-tuple-element.167) | copy-start | bytes 9220
  (66 other events, 255.1 us)
Sparse Core Ops, SparseCore 0:
  10.4 41.0 all-gather.6
  53.7 37.2 all-gather.8
  93.3 37.2 all-gather.10
  132.8 37.2 all-gather.12
  172.2 52.1 all-gather.14
  226.6 51.7 all-gather.16
  315.1 56.6 reduce-scatter.12
  375.4 57.1 reduce-scatter.10
  436.2 57.1 reduce-scatter.6
  496.8 56.9 reduce-scatter.8
  557.6 74.6 reduce-scatter.14
  636.5 74.6 reduce-scatter.16
  713.9 36.9 all-reduce.3
where the time goes:
time: 785 us; the launch traced here: 776 us
  waiting for transfers between devices  405 us (52%)
  matrix products  162 us (21%)
  blocking collectives  83.6 us (11%)
  local copies, waits for them, and re-layouts  65.2 us (8%)
  other arithmetic  42.9 us (5%)
  between operations  16.1 us (2%)
    reduce_scatter x1, waiting for transfers between devices, body(): lax.psum_scatter(out_weight_grad.astype(jnp.bfloat16), 'wide', scatter_di...  78.9 us
    reduce_scatter x1, waiting for transfers between devices, body(): lax.psum_scatter(in_weight_grad.astype(jnp.bfloat16), 'wide', scatter_dim...  78.6 us
    reduce_scatter x1, waiting for transfers between devices, body(): lax.psum_scatter(q_weight_grad.astype(jnp.bfloat16), 'wide', scatter_dime...  60.8 us
    reduce_scatter x1, waiting for transfers between devices, body(): lax.psum_scatter(k_weight_grad.astype(jnp.bfloat16), 'wide', scatter_dime...  60.5 us
    dot_general x6, matrix products, plain_product(): return jnp.dot(left, right, preferred_element_type=jnp.float32)  59 us
    all_gather x1, waiting for transfers between devices, body(): lax.all_gather(in_weight, 'wide', axis=0, tiled=True)  48.2 us
    psum x1, blocking collectives, body(): counts = lax.psum(local_counts, ('wide', 'narrow'))  42.4 us
    dot_general x6, matrix products, product_right_t(): lax.dot_general(left, right, (((1,), (1,)), ((), ())), preferred_element_...  41.2 us
  transfers between devices with their start and end apart: 13, of which 10 were waited for; matrix products, arithmetic and copies ran while one was open for 28% of the time, Pallas kernels for 0%

commit v1 on v0

--- a/solution.py
+++ b/solution.py
@@ -223,18 +223,21 @@
         (grad_resid + grad_x_norm).astype(jnp.bfloat16).reshape(row_local, slot_total, width_all)
     )
     summed_vectors = lax.psum(
-        (
-            norm1_gain_grad,
-            norm1_bias_grad,
-            q_bias_grad,
-            v_bias_grad,
-            o_bias_grad,
-            norm2_gain_grad,
-            norm2_bias_grad,
-            in_bias_grad,
-            out_bias_grad,
+        lax.psum(
+            (
+                norm1_gain_grad,
+                norm1_bias_grad,
+                q_bias_grad,
+                v_bias_grad,
+                o_bias_grad,
+                norm2_gain_grad,
+                norm2_bias_grad,
+                in_bias_grad,
+                out_bias_grad,
+            ),
+            "narrow",
         ),
-        ("wide", "narrow"),
+        "wide",
     )
     row_pieces = (
         lax.psum_scatter(

time: 785 us -> 811 us (1.033)
  blocking collectives: 83.6 us -> 110 us
    psum x0 -> x1, blocking collectives: none -> 58.4 us  [body(): lax.psum(lax.psum((norm1_gain_grad, norm1_bias_grad, q_bias_grad, v_bias_...]
    psum x1, blocking collectives: 41.2 us -> 8.98 us  [body(): lax.psum((norm1_gain_grad, norm1_bias_grad, q_bias_grad, v_bias_grad, o_b...]
  transfers between devices with their start and end apart: 13 -> 13, of which waited for: 10 -> 10; matrix products, arithmetic and copies ran while one was open for 28% -> 27% of each run, Pallas kernels for 0% -> 0%
where the time goes in v1:
time: 811 us; the launch traced here: 802 us
  waiting for transfers between devices  405 us (50%)
  matrix products  162 us (20%)
  blocking collectives  110 us (14%)
  local copies, waits for them, and re-layouts  65.1 us (8%)
  other arithmetic  42.9 us (5%)
  between operations  16.1 us (2%)
    reduce_scatter x1, waiting for transfers between devices, body(): lax.psum_scatter(out_weight_grad.astype(jnp.bfloat16), 'wide', scatter_di...  78.9 us
    reduce_scatter x1, waiting for transfers between devices, body(): lax.psum_scatter(in_weight_grad.astype(jnp.bfloat16), 'wide', scatter_dim...  78.5 us
    reduce_scatter x1, waiting for transfers between devices, body(): lax.psum_scatter(q_weight_grad.astype(jnp.bfloat16), 'wide', scatter_dime...  60.7 us
    reduce_scatter x1, waiting for transfers between devices, body(): lax.psum_scatter(k_weight_grad.astype(jnp.bfloat16), 'wide', scatter_dime...  60.5 us
    dot_general x6, matrix products, plain_product(): return jnp.dot(left, right, preferred_element_type=jnp.float32)  59 us
    psum x1, blocking collectives, body(): lax.psum(lax.psum((norm1_gain_grad, norm1_bias_grad, q_bias_grad, v_bias_...  58.4 us
    all_gather x1, waiting for transfers between devices, body(): lax.all_gather(in_weight, 'wide', axis=0, tiled=True)  48.2 us
    psum x1, blocking collectives, body(): counts = lax.psum(local_counts, ('wide', 'narrow'))  42.4 us
  transfers between devices with their start and end apart: 13, of which 10 were waited for; matrix products, arithmetic and copies ran while one was open for 27% of the time, Pallas kernels for 0%

profile of v1, /device:TPU:0, one launch (start us, length us, event | category | flops | bytes accessed | tf_op | source)
XLA Modules:
  0.0 802.1 jit_solution(15726784548656234792)
XLA Ops:
  18.4 42.4 %psum.175 = s32[3]{0:T(128)S(1)} all-reduce(s32[3]{0:T(128)S(1)} %pad_add_fusion), channel_id=1, replica_groups=mesh['wide'=16,'narrow'=2] {'wide','narrow'}, use_global_device_ids=true, to_apply=%region_12.13 | all-reduce | flops 3 | bytes 24 | tf_op jit(solution)/shard_map/psum | solution.py:125
  76.5 14.6 %all-gather.9.cloned.1.call-done = bf16[768,768]{1,0:T(8,128)(2,1)} async-done(((bf16[48,768]{1,0:T(8,128)(2,1)}), bf16[768,768]{1,0:T(8,128)(2,1)}) %all-gather.9.cloned.1.call-update) | async-done | bytes 1179664 | tf_op jit(solution)/shard_map/all_gather | solution.py:138
  98.5 32.1 %all-gather.11.cloned.1.call-done = bf16[768,768]{1,0:T(8,128)(2,1)} async-done(((bf16[48,768]{1,0:T(8,128)(2,1)}), bf16[768,768]{1,0:T(8,128)(2,1)}) %all-gather.11.cloned.1.call-update) | async-done | bytes 1179664 | tf_op jit(solution)/shard_map/all_gather | solution.py:139
  146.4 16.5 %while.26 = (s32[]{:T(128)}, bf16[2,2,256,12,64]{2,1,0,4,3:T(2,128)(2,1)}, f32[2,2,12,256,1]{3,2,1,4,0:T(8,128)}, bf16[2,2,256,12,64]{2,4,3,1,0:T(8,128)(2,1)}, ...) while((s32[]{:T(128)}, ...), condition=%wide.region_5.6_spmd, body=%wide.region_2.5_spmd.sunk | while | flops 422373888 | bytes 30772356 | solution.py:146
  176.2 48.2 %all-gather.15.cloned.1.call-done = bf16[768,3072]{1,0:T(8,128)(2,1)} async-done(((bf16[48,3072]{1,0:T(8,128)(2,1)}), bf16[768,3072]{1,0:T(8,128)(2,1)}) %all-gather.15.cloned.1.call-update) | async-done | bytes 4718608 | tf_op jit(solution)/shard_map/all_gather | solution.py:160
  224.4 38.2 %multiply_convert_fusion.3 = (bf16[1024,3072]{1,0:T(8,128)(2,1)}, f32[1024,3072]{1,0:T(8,128)}, f32[1024,3072]{1,0:T(8,128)}) fusion(f32[3072]{0:T(1024)S(1)} %copy-done.55, bf16[768,3072]{1,0:T(8,128)(2,1)} %all-gather.15.cloned.1.call-done, f32[1024,768]{1,0:T(8,128)} %copy-done.12, f32[768]{0:T(1024)S(1)} %copy-done.59, f32[768]{0:T(1024)S(1)} %copy-done.48, ...), kind=kOutput, calls=%fused_computation.74 | convolution fusion | flops 5043388416 | bytes 39348224 | tf_op jit(solution)/shard_map/dot_general | solution.py:24
  262.6 15.8 %all-gather.17.cloned.1.call-done = bf16[3072,768]{1,0:T(8,128)(2,1)} async-done(((bf16[192,768]{1,0:T(8,128)(2,1)}), bf16[3072,768]{1,0:T(8,128)(2,1)}) %all-gather.17.cloned.1.call-update) | async-done | bytes 4718608 | tf_op jit(solution)/shard_map/all_gather | solution.py:161
  278.4 18.9 %convert_reduce_fusion = (f32[3072]{0:T(1024)}, bf16[1024,3072]{1,0:T(8,128)(2,1)}) fusion(f32[1024,3072]{1,0:T(8,128)} %get-tuple-element.240, bf16[1024,768]{1,0:T(8,128)(2,1)} %fusion.76, bf16[3072,768]{1,0:T(8,128)(2,1)} %all-gather.17.cloned.1.call-done, f32[1024,3072]{1,0:T(8,128)} %get-tuple-element.253, f32[3072]{0:T(1024)S(1)} %copy-done.55), kind=kOutput, calls=%fused_computation.72 | convolution fusion | flops 4885312512 | bytes 37773312 | tf_op jit(solution)/shard_map/dot_general | solution.py:34
  297.2 10.2 %multiply_reduce_fusion.1 = (f32[768]{0:T(1024)}, f32[1024]{0:T(1024)S(1)}, f32[768]{0:T(1024)}, f32[1024,768]{1,0:T(8,128)S(1)}) fusion(f32[1024,768]{1,0:T(8,128)S(1)} %copy-done.13, f32[1024]{0:T(1024)S(1)} %fusion.78, f32[1024]{0:T(1024)S(1)} %broadcast_multiply_fusion, f32[768]{0:T(1024)S(1)} %copy-done.48, ...), kind=kOutput, calls=%fused_computation.115 | convolution fusion | flops 4838126592 | bytes 17323008 | tf_op jit(solution)/shard_map/dot_general | solution.py:34
  327.5 30.1 %while.27 = (s32[]{:T(128)}, bf16[2,2,256,12,64]{2,4,3,1,0:T(8,128)(2,1)}, bf16[2,2,256,12,64]{2,1,0,4,3:T(2,128)(2,1)}, bf16[2,2,256,12,64]{2,4,3,1,0:T(8,128)(...) while((s32[]{:T(128)}, ...), condition=%wide.region_17.18_spmd, body=%wide.region_15.17_spmd.sunk | while | flops 1032645120 | bytes 109375376 | solution.py:195
  362.0 4.5 convolution_convert_fusion.5
  370.5 4.5 convolution_convert_fusion.7
  377.5 4.5 convolution_convert_fusion.6
  382.0 10.0 %convolution_convert_fusion.1 = bf16[768,3072]{1,0:T(8,128)(2,1)} fusion(bf16[1024,3072]{1,0:T(8,128)(2,1)} %get-tuple-element.257, f32[1024,768]{1,0:T(8,128)S(1)} %copy-done.14, f32[768]{0:T(1024)S(1)} %copy-done.60, f32[768]{0:T(1024)S(1)} %copy-done.48, f32[1024]{0:T(1024)S(1)} %fusion.78, f32[1024]{0:T(1024)S(1)} %broadcast_multiply_fusion), kind=kOutput, calls=%fused_computation.89 | convolution fusion | flops 4838129664 | bytes 14170112 | tf_op jit(solution)/shard_map/dot_general | solution.py:28
  393.4 10.0 %convolution_convert_fusion = bf16[3072,768]{1,0:T(8,128)(2,1)} fusion(bf16[1024,3072]{1,0:T(8,128)(2,1)} %get-tuple-element.239, bf16[1024,768]{1,0:T(8,128)(2,1)S(1)} %copy-done.24), kind=kOutput, calls=%fused_computation.88 | convolution fusion | flops 4834197504 | bytes 12582912 | tf_op jit(solution)/shard_map/dot_general | solution.py:28
  417.5 6.1 add_convert_fusion.2
  423.6 8.8 %reduce-scatter.11.cloned.1.call-done = bf16[48,768]{1,0:T(8,128)(2,1)} async-done(((bf16[768,768]{1,0:T(8,128)(2,1)}), bf16[48,768]{1,0:T(8,128)(2,1)}) %reduce-scatter.11.cloned.1.call-update) | async-done | bytes 73744 | tf_op jit(solution)/shard_map/reduce_scatter | solution.py:249
  432.4 60.7 %reduce-scatter.7.cloned.1.call-done = bf16[48,768]{1,0:T(8,128)(2,1)} async-done(((bf16[768,768]{1,0:T(8,128)(2,1)}), bf16[48,768]{1,0:T(8,128)(2,1)}) %reduce-scatter.7.cloned.1.call-update) | async-done | bytes 73744 | tf_op jit(solution)/shard_map/reduce_scatter | solution.py:243
  493.1 60.5 %reduce-scatter.9.cloned.1.call-done = bf16[48,768]{1,0:T(8,128)(2,1)} async-done(((bf16[768,768]{1,0:T(8,128)(2,1)}), bf16[48,768]{1,0:T(8,128)(2,1)}) %reduce-scatter.9.cloned.1.call-update) | async-done | bytes 73744 | tf_op jit(solution)/shard_map/reduce_scatter | solution.py:246
  553.6 78.5 %reduce-scatter.15.cloned.1.call-done = bf16[48,3072]{1,0:T(8,128)(2,1)} async-done(((bf16[768,3072]{1,0:T(8,128)(2,1)}), bf16[48,3072]{1,0:T(8,128)(2,1)}) %reduce-scatter.15.cloned.1.call-update) | async-done | bytes 294928 | tf_op jit(solution)/shard_map/reduce_scatter | solution.py:255
  632.2 78.9 %reduce-scatter.17.cloned.1.call-done = bf16[192,768]{1,0:T(8,128)(2,1)} async-done(((bf16[3072,768]{1,0:T(8,128)(2,1)}), bf16[192,768]{1,0:T(8,128)(2,1)}) %reduce-scatter.17.cloned.1.call-update) | async-done | bytes 294928 | tf_op jit(solution)/shard_map/reduce_scatter | solution.py:258
  713.6 9.0 %all-reduce.1 = (f32[768]{0:T(1024)S(1)}, f32[768]{0:T(1024)S(1)}, f32[768]{0:T(1024)S(1)}, f32[768]{0:T(1024)S(1)}, f32[768]{0:T(1024)S(1)}, /*index=5*/f32[768...) all-reduce(f32[768]{0:T(1024)S(1)} %get-tuple-element.165, ...), channel_id=1, replica_groups=mesh['wide'=16,'narrow'=2] {'narrow'}, use_global_device_ids=true, to_apply=%region_21.22 | all-reduce | flops 9216 | bytes 73728 | tf_op jit(solution)/shard_map/psum | solution.py:226
  722.6 58.4 %all-reduce = (f32[768]{0:T(1024)}, f32[768]{0:T(1024)}, f32[768]{0:T(1024)}, f32[768]{0:T(1024)}, f32[768]{0:T(1024)}, /*index=5*/f32[768]{0:T(1024)}, f32[768]{0:T(1024)}, f32[3072]{0:T(1024)}, f32[768]{0:T(1024)}) all-reduce(f32[768]{0:T(1024)S(1)} %get-tuple-element.220, ...), channel_id=1, replica_groups=mesh['wide'=16,'narrow'=2] {'wide'}, use_global_device_ids=true, to_apply=%region_22.23 | all-reduce | flops 9216 | bytes 73728 | tf_op jit(solution)/shard_map/psum | solution.py:225
  781.0 4.5 add_convert_fusion.1
  (302 shorter events, 165.9 us)
Async XLA Ops:
  7.2 56.8 %copy-start.38 = (s32[4,256]{1,0:T(4,128)S(1)}, s32[4,256]{1,0:T(4,128)}, u32[]{:S(2)}) copy-start(s32[4,256]{1,0:T(4,128)} %param.26) | copy-start | bytes 12292
  7.2 56.9 %copy-start.32 = (f32[768]{0:T(1024)S(1)}, f32[768]{0:T(1024)}, u32[]{:S(2)}) copy-start(f32[768]{0:T(1024)} %param.29) | copy-start | bytes 9220
  7.2 56.9 %copy-start.44 = (f32[768]{0:T(1024)S(1)}, f32[768]{0:T(1024)}, u32[]{:S(2)}) copy-start(f32[768]{0:T(1024)} %param.30) | copy-start | bytes 9220
  7.3 61.0 %all-gather.7.cloned.1.call-start = ((), (), s32[]{:S(2)}) async-start(), calls=%async_computation.6 | async-start | bytes 1253376 | tf_op jit(solution)/shard_map/all_gather | solution.py:140
  8.0 83.0 %all-gather.9.cloned.1.call-start = ((), (), s32[]{:S(2)}) async-start(), calls=%async_computation.7 | async-start | bytes 1253376 | tf_op jit(solution)/shard_map/all_gather | solution.py:138
  8.7 121.9 %all-gather.11.cloned.1.call-start = ((), (), s32[]{:S(2)}) async-start(), calls=%async_computation.8 | async-start | bytes 1253376 | tf_op jit(solution)/shard_map/all_gather | solution.py:139
  9.5 160.6 %all-gather.13.cloned.1.call-start = ((), (), s32[]{:S(2)}) async-start(), calls=%async_computation.9 | async-start | bytes 1253376 | tf_op jit(solution)/shard_map/all_gather | solution.py:141
  10.1 214.4 %all-gather.15.cloned.1.call-start = ((), (), s32[]{:S(2)}) async-start(), calls=%async_computation.10 | async-start | bytes 5013504 | tf_op jit(solution)/shard_map/all_gather | solution.py:160
  10.6 267.7 %all-gather.17.cloned.1.call-start = ((), (), s32[]{:S(2)}) async-start(), calls=%async_computation.11 | async-start | bytes 5013504 | tf_op jit(solution)/shard_map/all_gather | solution.py:161
  11.2 412.4 %reduce-scatter.13.cloned.1.call-start = ((), (), s32[]{:S(2)}) async-start(), calls=%async_computation.15 | async-start | bytes 1253376 | tf_op jit(solution)/shard_map/reduce_scatter | solution.py:252
  15.7 50.9 %copy-start.36 = (f32[1024]{0:T(1024)}, f32[1024]{0:T(1024)S(1)}, u32[]{:S(2)}) copy-start(f32[1024]{0:T(1024)S(1)} %rsqrt.25) | copy-start | bytes 12292
  15.7 50.9 %copy-start.34 = (f32[1,2,4,128]{3,1,2,0:T(2,128)}, f32[1,2,4,128]{3,1,2,0:T(2,128)S(1)}, u32[]{:S(2)}) copy-start(f32[1,2,4,128]{3,1,2,0:T(2,128)S(1)} %copy.77) | copy-start | bytes 12292
  174.0 50.4 %copy-start.48 = (f32[768]{0:T(1024)S(1)}, f32[768]{0:T(1024)}, u32[]{:S(2)}) copy-start(f32[768]{0:T(1024)} %param.38) | copy-start | bytes 9220
  174.0 50.4 %copy-start.55 = (f32[3072]{0:T(1024)S(1)}, f32[3072]{0:T(1024)}, u32[]{:S(2)}) copy-start(f32[3072]{0:T(1024)} %param.41) | copy-start | bytes 36868
  174.0 50.4 %copy-start.59 = (f32[768]{0:T(1024)S(1)}, f32[768]{0:T(1024)}, u32[]{:S(2)}) copy-start(f32[768]{0:T(1024)} %param.39) | copy-start | bytes 9220
  314.8 117.6 %reduce-scatter.11.cloned.1.call-start = ((), (), s32[]{:S(2)}) async-start(), calls=%async_computation.14 | async-start | bytes 1253376 | tf_op jit(solution)/shard_map/reduce_scatter | solution.py:249
  366.4 126.7 %reduce-scatter.7.cloned.1.call-start = ((), (), s32[]{:S(2)}) async-start(), calls=%async_computation.12 | async-start | bytes 1253376 | tf_op jit(solution)/shard_map/reduce_scatter | solution.py:243
  375.1 178.6 %reduce-scatter.9.cloned.1.call-start = ((), (), s32[]{:S(2)}) async-start(), calls=%async_computation.13 | async-start | bytes 1253376 | tf_op jit(solution)/shard_map/reduce_scatter | solution.py:246
  381.9 250.2 %reduce-scatter.15.cloned.1.call-start = ((), (), s32[]{:S(2)}) async-start(), calls=%async_computation.16 | async-start | bytes 5013504 | tf_op jit(solution)/shard_map/reduce_scatter | solution.py:255
  392.0 319.0 %reduce-scatter.17.cloned.1.call-start = ((), (), s32[]{:S(2)}) async-start(), calls=%async_computation.17 | async-start | bytes 5013504 | tf_op jit(solution)/shard_map/reduce_scatter | solution.py:258
  403.5 382.0 %all-reduce.5.cloned.1.call-start = ((), (), s32[]{:S(2)}) async-start(), calls=%async_computation.18 | async-start | bytes 1769472 | tf_op jit(solution)/shard_map/psum | solution.py:263
  423.6 290.0 %copy-start.45 = (f32[3072]{0:T(1024)S(1)}, f32[3072]{0:T(1024)}, u32[]{:S(2)}) copy-start(f32[3072]{0:T(1024)} %get-tuple-element.256) | copy-start | bytes 36868
  423.6 290.0 %copy-start.50 = (f32[768]{0:T(1024)S(1)}, f32[768]{0:T(1024)}, u32[]{:S(2)}) copy-start(f32[768]{0:T(1024)} %get-tuple-element.163) | copy-start | bytes 9220
  423.6 290.0 %copy-start.51 = (f32[768]{0:T(1024)S(1)}, f32[768]{0:T(1024)}, u32[]{:S(2)}) copy-start(f32[768]{0:T(1024)} %get-tuple-element.167) | copy-start | bytes 9220
  (66 other events, 255.0 us)
Sparse Core Ops, SparseCore 0:
  10.4 41.0 all-gather.6
  53.7 37.2 all-gather.8
  93.3 37.2 all-gather.10
  132.8 37.2 all-gather.12
  172.2 52.1 all-gather.14
  226.6 51.7 all-gather.16
  314.9 56.6 reduce-scatter.12
  375.2 57.1 reduce-scatter.10
  436.0 57.0 reduce-scatter.6
  496.6 56.9 reduce-scatter.8
  557.5 74.6 reduce-scatter.14
  636.4 74.6 reduce-scatter.16
  713.7 36.4 all-reduce.4
